TPU v7x, 32 devices: a whole 2x2x4 slice. The times are simulated.
32 devices in a mesh: item: 8 (over y, x, core), dp: 4 (over z).
Axes of the slice: x: 2, y: 2, z: 4, core: 2. Of those that a mesh axis runs over, the one named last changes fastest.
Arguments:
- hidden_states: bfloat16 [32768, 512], P(('item', 'dp'))
- item_table: bfloat16 [4096, 512], P('item'), may hold values from -0.25 to 0.25
- cand_local: int32 [64], replicated, may hold values from 0 to 511
- log_sample: float32 [64], replicated, may hold values from -14 to -4
- target_slot: int32 [32768], P(('item', 'dp')), may hold values from 0 to 63
- loss_weight: float32 [32768], P(('item', 'dp')), may hold values from -6 to 6
Outputs:
- grad_hidden: bfloat16 [32768, 512], P(('item', 'dp'))
- grad_table: float32 [4096, 512], P('item')
Inputs may be any that keep to these rules, and one draw needn't show every extreme that they name: Candidate slot s belongs to the item shard s // 8; cand_local counts rows within that shard, and a row may be sampled more than once.
All inputs are finite; a program needn't handle non-finite values.
Results may differ from a plain program's by a relative error of at most 0.0049.
Values may be sent and summed in bfloat16 or wider, within the bound.
No kernel may reach another device: no remote copies, remote signals or barrier semaphores. Data moves between devices by JAX's collectives and lax.ppermute only.
A program may use at most 64 MiB of HBM per device.

v0:
```python
import math
import jax
import jax.numpy as jnp
from jax import lax
from jax.sharding import PartitionSpec as P


def on_device(hidden_states, item_table, cand_local, log_sample, target_slot, loss_weight):
    owners = lax.axis_size("item")
    total_cands = log_sample.shape[0]
    per_owner = total_cands // owners
    my_index = lax.axis_index("item")
    my_local = lax.dynamic_slice_in_dim(cand_local, my_index * per_owner, per_owner)
    my_rows = item_table[my_local]
    cand_rows = lax.all_gather(my_rows, "item", axis=0, tiled=True)
    slots = jnp.arange(total_cands, dtype=jnp.int32)
    tok_rows = hidden_states.shape[0]
    width = hidden_states.shape[1]
    block = math.gcd(tok_rows, 512)
    count = tok_rows // block
    states = hidden_states.reshape(count, block, width)
    targets = target_slot.reshape(count, block)
    weights = loss_weight.reshape(count, block)

    def step(total, inputs):
        rows, tgt, wts = inputs
        logits = (
            jnp.dot(rows, cand_rows.T, preferred_element_type=jnp.float32) - log_sample[None, :]
        )
        probs = jax.nn.softmax(logits, axis=1)
        onehot = (tgt[:, None] == slots[None, :]).astype(jnp.float32)
        grad_logits = (wts[:, None] * (probs - onehot)).astype(jnp.bfloat16)
        grad_rows = jnp.dot(grad_logits, cand_rows, preferred_element_type=jnp.float32).astype(
            jnp.bfloat16
        )
        total = total + jnp.dot(grad_logits.T, rows, preferred_element_type=jnp.float32)
        return (total, grad_rows)

    partial_grad, grad_blocks = lax.scan(
        step, jnp.zeros((total_cands, width), jnp.float32), (states, targets, weights)
    )
    grad_hidden = grad_blocks.reshape(tok_rows, width)
    owned = lax.psum_scatter(partial_grad, "item", scatter_dimension=0, tiled=True)
    owned = lax.psum(owned, "dp")
    table_rows = item_table.shape[0]
    placing = (my_local[:, None] == jnp.arange(table_rows, dtype=jnp.int32)[None, :]).astype(
        jnp.float32
    )
    grad_table = jnp.dot(
        placing.T, owned, preferred_element_type=jnp.float32, precision=lax.Precision.HIGHEST
    )
    return (grad_hidden, grad_table)


def solution(mesh):
    placed = (
        P(("item", "dp"), None),
        P("item", None),
        P(),
        P(),
        P(("item", "dp")),
        P(("item", "dp")),
    )
    return jax.shard_map(
        on_device,
        mesh=mesh,
        in_specs=placed,
        out_specs=(P(("item", "dp"), None), P("item", None)),
        check_vma=False,
    )
```

profile of v0, /device:TPU:0, one launch (start us, length us, event | category | flops | bytes accessed | tf_op | source)
XLA Modules:
  0.0 87.7 jit_solution(3988291975070287816)
XLA Ops:
  7.2 0.0 copy-start
  7.2 0.0 reduce-scatter.2.cloned.1.call-start
  7.3 0.0 copy-start.6
  7.3 0.7 copy-done.6
  8.0 0.1 compare_select_fusion
  8.0 0.2 copy-done
  8.2 0.6 gather_fusion
  8.8 0.0 copy-start.4
  8.8 10.7 %all-gather = bf16[64,512]{1,0:T(8,128)(2,1)S(1)} all-gather(bf16[8,512]{1,0:T(8,128)(2,1)S(1)} %gather_fusion), channel_id=2, replica_groups=mesh['item'=8,'dp'=4] {'item'}, dimensions={0}, use_global_device_ids=true | all-gather | bytes 73728 | tf_op jit(solution)/shard_map/all_gather | solution.py:15
  19.5 0.0 copy-done.4
  19.5 0.0 copy-start.5
  19.6 0.7 copy-done.5
  20.2 0.0 copy-start.3
  20.2 0.7 copy-done.3
  20.9 4.2 %while.13 = (s32[]{:T(128)}, f32[64,512]{1,0:T(8,128)S(1)}, bf16[2,512,512]{2,1,0:T(8,128)(2,1)S(1)}, f32[2,512]{1,0:T(2,128)S(1)}, bf16[2,512,512]{2,1,0:T(8,12...) while((s32[]{:T(128)}, f32[64,512]{1,0:T(8,128)S(1)}, ...), condition=%wide.region_3.4_spmd.clone, body=%wide.region_0.3_spmd.clone.sunk | while | flops 101579776 | bytes 6716315 | solution.py:39
  20.9 0.0 copy-start.1
  20.9 1.4 %fusion.26 = (f32[512]{0:T(512)S(1)}, f32[512,64]{0,1:T(8,128)S(1)}) fusion(f32[64]{0:T(128)S(1)} %get-tuple-element.180, bf16[64,512]{1,0:T(8,128)(2,1)S(1)} %get-tuple-element.179, bf16[2,512,512]{2,1,0:T(8,128)(2,1)} %get-tuple-element.178, s32[]{:T(128)} %get-tuple-element.164), kind=kOutput, calls=%fused_computation.24.clone.1 | convolution fusion | flops 33619456 | bytes 723712 | tf_op jit(solution)/shard_map/while/body/eval_jaxpr/dot_general | solution.py:28
  22.4 0.3 fusion.28
  22.8 0.0 copy-done.1
  22.8 0.2 convolution_add_fusion.2
  23.0 0.0 copy-start.1
  23.0 1.4 %fusion.26 = (f32[512]{0:T(512)S(1)}, f32[512,64]{0,1:T(8,128)S(1)}) fusion(f32[64]{0:T(128)S(1)} %get-tuple-element.180, bf16[64,512]{1,0:T(8,128)(2,1)S(1)} %get-tuple-element.179, bf16[2,512,512]{2,1,0:T(8,128)(2,1)} %get-tuple-element.178, s32[]{:T(128)} %get-tuple-element.164), kind=kOutput, calls=%fused_computation.24.clone.1 | convolution fusion | flops 33619456 | bytes 723712 | tf_op jit(solution)/shard_map/while/body/eval_jaxpr/dot_general | solution.py:28
  24.5 0.3 fusion.28
  24.9 0.0 copy-done.1
  24.9 0.2 convolution_add_fusion.2
  25.1 0.0 copy-start.2
  25.2 0.0 copy-start.7
  25.2 0.6 copy-done.2
  25.8 0.0 reduce-scatter.2.cloned.1.call-update
  25.8 34.0 %reduce-scatter.2.cloned.1.call-done = f32[8,512]{1,0:T(8,128)} async-done(((f32[64,512]{1,0:T(8,128)}), f32[8,512]{1,0:T(8,128)}) %reduce-scatter.2.cloned.1.call-update) | async-done | bytes 16400 | tf_op jit(solution)/shard_map/reduce_scatter | solution.py:43
  59.8 19.4 %psum.7 = f32[8,512]{1,0:T(8,128)S(1)} all-reduce(f32[8,512]{1,0:T(8,128)} %reduce-scatter.2.cloned.1.call-done), channel_id=1, replica_groups=mesh['item'=8,'dp'=4] {'dp'}, use_global_device_ids=true, to_apply=%region_5.6 | all-reduce | flops 4096 | bytes 32768 | tf_op jit(solution)/shard_map/psum | solution.py:44
  79.2 1.7 %fusion.11 = f32[512,512]{1,0:T(8,128)} fusion(f32[8,512]{1,0:T(8,128)S(1)} %psum.7, s32[8]{0:T(128)S(1)} %get-tuple-element.98), kind=kOutput, calls=%fused_computation.20 | convolution fusion | flops 25169920 | bytes 1064992 | tf_op jit(solution)/shard_map/dot_general | solution.py:49
  80.8 0.0 copy-done.7
  (11 shorter events, 0.2 us)
Async XLA Ops:
  7.2 1.1 %copy-start = (bf16[512,512]{1,0:T(8,128)(2,1)S(1)}, bf16[512,512]{1,0:T(8,128)(2,1)}, u32[]{:S(2)}) copy-start(bf16[512,512]{1,0:T(8,128)(2,1)} %param.9) | copy-start | bytes 1572868
  7.2 52.6 %reduce-scatter.2.cloned.1.call-start = ((), (), s32[]{:S(2)}) async-start(), calls=%async_computation.1 | async-start | bytes 147456 | tf_op jit(solution)/shard_map/reduce_scatter | solution.py:43
  7.3 0.7 copy-start.6
  8.8 10.7 %copy-start.4 = (f32[1024]{0:T(1024)S(1)}, f32[1024]{0:T(1024)}, u32[]{:S(2)}) copy-start(f32[1024]{0:T(1024)} %param.13) | copy-start | bytes 12292
  19.5 0.7 copy-start.5
  20.2 0.7 copy-start.3
  20.9 1.9 %copy-start.1 = (bf16[2,512,512]{2,1,0:T(8,128)(2,1)S(1)}, bf16[2,512,512]{2,1,0:T(8,128)(2,1)}, u32[]{:S(2)}) copy-start(bf16[2,512,512]{2,1,0:T(8,128)(2,1)} %get-tuple-element.178) | copy-start | bytes 3145732 | tf_op jit(solution)/shard_map/while
  23.0 1.9 %copy-start.1 = (bf16[2,512,512]{2,1,0:T(8,128)(2,1)S(1)}, bf16[2,512,512]{2,1,0:T(8,128)(2,1)}, u32[]{:S(2)}) copy-start(bf16[2,512,512]{2,1,0:T(8,128)(2,1)} %get-tuple-element.178) | copy-start | bytes 3145732 | tf_op jit(solution)/shard_map/while
  25.1 0.7 copy-start.2
  25.2 55.7 %copy-start.7 = (bf16[2,512,512]{2,1,0:T(8,128)(2,1)}, bf16[2,512,512]{2,1,0:T(8,128)(2,1)S(1)}, u32[]{:S(2)}) copy-start(bf16[2,512,512]{2,1,0:T(8,128)(2,1)S(1)} %get-tuple-element.50) | copy-start | bytes 3145732
Sparse Core Ops, SparseCore 0:
  26.0 33.8 reduce-scatter.1
where the time goes:
time: 88 us; the launch traced here: 87.7 us
  waiting for transfers between devices  34 us (39%)
  blocking collectives  30.1 us (34%)
  between operations  14.1 us (16%)
  matrix products  5.64 us (6%)
  local copies, waits for them, and re-layouts  3.5 us (4%)
    reduce_scatter x1, waiting for transfers between devices, on_device(): lax.psum_scatter(partial_grad, 'item', scatter_dimension=0, tiled=True)  34 us
    psum x1, blocking collectives, on_device(): owned = lax.psum(owned, 'dp')  19.4 us
    all_gather x1, blocking collectives, on_device(): cand_rows = lax.all_gather(my_rows, 'item', axis=0, tiled=True)  10.7 us
    unnamed x14, local copies, waits for them, and re-layouts  2.87 us
    dot_general x2, matrix products, step(): jnp.dot(rows, cand_rows.T, preferred_element_type=jnp.float32)  2.86 us
  transfers between devices with their start and end apart: 1, of which 1 were waited for; matrix products, arithmetic and copies ran while one was open for 0% of the time, Pallas kernels for 0%

commit v1 on v0

--- a/solution.py
+++ b/solution.py
@@ -12,7 +12,9 @@
     my_index = lax.axis_index("item")
     my_local = lax.dynamic_slice_in_dim(cand_local, my_index * per_owner, per_owner)
     my_rows = item_table[my_local]
-    cand_rows = lax.all_gather(my_rows, "item", axis=0, tiled=True)
+    cand_rows = jnp.concatenate(
+        lax.all_to_all(jnp.stack([my_rows] * lax.axis_size("item")), "item", 0, 0), axis=0
+    )
     slots = jnp.arange(total_cands, dtype=jnp.int32)
     tok_rows = hidden_states.shape[0]
     width = hidden_states.shape[1]

time: 88 us -> 86.5 us (0.983)
  blocking collectives: 30.1 us -> 19.3 us
  starting transfers between devices: 0.04 us -> 5.24 us
  waiting for transfers between devices: 34 us -> 36.7 us
  local copies, waits for them, and re-layouts: 3.5 us -> 4.82 us
    all_gather x1 -> x0, blocking collectives: 10.7 us -> none  [on_device(): cand_rows = lax.all_gather(my_rows, 'item', axis=0, tiled=True)]
    all_to_all x0 -> x1, starting transfers between devices: none -> 5.2 us  [on_device(): lax.all_to_all(jnp.stack([my_rows] * lax.axis_size('item')), 'item', 0, 0)]
    all_to_all x0 -> x1, waiting for transfers between devices: none -> 3.64 us  [on_device(): lax.all_to_all(jnp.stack([my_rows] * lax.axis_size('item')), 'item', 0, 0)]
    reduce_scatter x1, waiting for transfers between devices: 34 us -> 33.1 us  [on_device(): lax.psum_scatter(partial_grad, 'item', scatter_dimension=0, tiled=True)]
  transfers between devices with their start and end apart: 1 -> 2, of which waited for: 1 -> 2; matrix products, arithmetic and copies ran while one was open for 0% -> 0% of each run, Pallas kernels for 0% -> 0%
where the time goes in v1:
time: 86.5 us; the launch traced here: 86.2 us
  waiting for transfers between devices  36.7 us (42%)
  blocking collectives  19.3 us (22%)
  between operations  14.1 us (16%)
  matrix products  5.64 us (7%)
  starting transfers between devices  5.24 us (6%)
  local copies, waits for them, and re-layouts  4.82 us (6%)
    reduce_scatter x1, waiting for transfers between devices, on_device(): lax.psum_scatter(partial_grad, 'item', scatter_dimension=0, tiled=True)  33.1 us
    psum x1, blocking collectives, on_device(): owned = lax.psum(owned, 'dp')  19.3 us
    all_to_all x1, starting transfers between devices, on_device(): lax.all_to_all(jnp.stack([my_rows] * lax.axis_size('item')), 'item', 0, 0)  5.2 us
    all_to_all x1, waiting for transfers between devices, on_device(): lax.all_to_all(jnp.stack([my_rows] * lax.axis_size('item')), 'item', 0, 0)  3.64 us
    unnamed x14, local copies, waits for them, and re-layouts  3.55 us
    dot_general x2, matrix products, step(): jnp.dot(rows, cand_rows.T, preferred_element_type=jnp.float32)  2.85 us
  transfers between devices with their start and end apart: 2, of which 2 were waited for; matrix products, arithmetic and copies ran while one was open for 0% of the time, Pallas kernels for 0%

profile of v1, /device:TPU:0, one launch (start us, length us, event | category | flops | bytes accessed | tf_op | source)
XLA Modules:
  0.0 86.2 jit_solution(12820022731517037253)
XLA Ops:
  7.2 0.0 copy-start
  7.2 0.0 copy-start.6
  7.2 0.7 copy-done.6
  7.9 0.1 compare_select_fusion
  8.0 0.2 copy-done
  8.2 0.6 gather_fusion
  8.8 0.6 stack.2
  9.4 5.2 %all-to-all-start = ((bf16[8,8,512]{2,1,0:T(8,128)(2,1)}), bf16[8,8,512]{2,1,0:T(8,128)(2,1)S(1)}, u32[]{:S(2)}, u32[]{:S(2)}) async-start(bf16[8,8,512]{2,1,0:T(8,128)(2,1)} %stack.2), calls=%async_computation | async-start | bytes 131072 | tf_op jit(solution)/shard_map/all_to_all | solution.py:16
  14.6 0.0 copy-start.4
  14.6 0.0 reduce-scatter.2.cloned.1.call-start
  14.7 0.6 copy-done.4
  15.3 0.0 copy-start.5
  15.3 0.7 copy-done.5
  16.0 3.6 %all-to-all-done = bf16[8,8,512]{2,1,0:T(8,128)(2,1)S(1)} async-done(((bf16[8,8,512]{2,1,0:T(8,128)(2,1)}), bf16[8,8,512]{2,1,0:T(8,128)(2,1)S(1)}, u32[]{:S(2)}, u32[]{:S(2)}) %all-to-all-start) | async-done | bytes 65568 | tf_op jit(solution)/shard_map/all_to_all | solution.py:16
  19.7 0.0 copy-start.3
  19.7 0.7 copy-done.3
  20.3 4.2 %while.13 = (s32[]{:T(128)}, f32[64,512]{1,0:T(8,128)S(1)}, bf16[2,512,512]{2,1,0:T(8,128)(2,1)S(1)}, f32[2,512]{1,0:T(2,128)S(1)}, bf16[2,512,512]{2,1,0:T(8,12...) while((s32[]{:T(128)}, f32[64,512]{1,0:T(8,128)S(1)}, ...), condition=%wide.region_3.4_spmd.clone, body=%wide.region_0.3_spmd.clone.sunk | while | flops 101579776 | bytes 6716315 | solution.py:41
  20.3 0.0 copy-start.1
  20.3 1.4 %fusion.26 = (f32[512]{0:T(512)S(1)}, f32[512,64]{0,1:T(8,128)S(1)}) fusion(f32[64]{0:T(128)S(1)} %get-tuple-element.180, bf16[64,512]{1,0:T(8,128)(2,1)S(1)} %get-tuple-element.179, bf16[2,512,512]{2,1,0:T(8,128)(2,1)} %get-tuple-element.178, s32[]{:T(128)} %get-tuple-element.164), kind=kOutput, calls=%fused_computation.24.clone.1 | convolution fusion | flops 33619456 | bytes 723712 | tf_op jit(solution)/shard_map/while/body/eval_jaxpr/dot_general | solution.py:30
  21.8 0.3 fusion.28
  22.2 0.0 copy-done.1
  22.2 0.2 convolution_add_fusion.2
  22.4 0.0 copy-start.1
  22.4 1.4 %fusion.26 = (f32[512]{0:T(512)S(1)}, f32[512,64]{0,1:T(8,128)S(1)}) fusion(f32[64]{0:T(128)S(1)} %get-tuple-element.180, bf16[64,512]{1,0:T(8,128)(2,1)S(1)} %get-tuple-element.179, bf16[2,512,512]{2,1,0:T(8,128)(2,1)} %get-tuple-element.178, s32[]{:T(128)} %get-tuple-element.164), kind=kOutput, calls=%fused_computation.24.clone.1 | convolution fusion | flops 33619456 | bytes 723712 | tf_op jit(solution)/shard_map/while/body/eval_jaxpr/dot_general | solution.py:30
  23.9 0.3 fusion.28
  24.3 0.0 copy-done.1
  24.3 0.2 convolution_add_fusion.2
  24.6 0.0 copy-start.2
  24.6 0.0 copy-start.7
  24.6 0.6 copy-done.2
  25.2 0.0 reduce-scatter.2.cloned.1.call-update
  25.2 33.1 %reduce-scatter.2.cloned.1.call-done = f32[8,512]{1,0:T(8,128)} async-done(((f32[64,512]{1,0:T(8,128)}), f32[8,512]{1,0:T(8,128)}) %reduce-scatter.2.cloned.1.call-update) | async-done | bytes 16400 | tf_op jit(solution)/shard_map/reduce_scatter | solution.py:45
  58.3 19.3 %psum.7 = f32[8,512]{1,0:T(8,128)S(1)} all-reduce(f32[8,512]{1,0:T(8,128)} %reduce-scatter.2.cloned.1.call-done), channel_id=1, replica_groups=mesh['item'=8,'dp'=4] {'dp'}, use_global_device_ids=true, to_apply=%region_5.6 | all-reduce | flops 4096 | bytes 32768 | tf_op jit(solution)/shard_map/psum | solution.py:46
  77.6 1.7 %fusion.11 = f32[512,512]{1,0:T(8,128)} fusion(f32[8,512]{1,0:T(8,128)S(1)} %psum.7, s32[8]{0:T(128)S(1)} %get-tuple-element.98), kind=kOutput, calls=%fused_computation.20 | convolution fusion | flops 25169920 | bytes 1064992 | tf_op jit(solution)/shard_map/dot_general | solution.py:51
  79.3 0.0 copy-done.7
  (11 shorter events, 0.2 us)
Async XLA Ops:
  7.2 1.1 %copy-start = (bf16[512,512]{1,0:T(8,128)(2,1)S(1)}, bf16[512,512]{1,0:T(8,128)(2,1)}, u32[]{:S(2)}) copy-start(bf16[512,512]{1,0:T(8,128)(2,1)} %param.9) | copy-start | bytes 1572868
  7.2 0.7 copy-start.6
  9.4 10.2 %all-to-all-start = ((bf16[8,8,512]{2,1,0:T(8,128)(2,1)}), bf16[8,8,512]{2,1,0:T(8,128)(2,1)S(1)}, u32[]{:S(2)}, u32[]{:S(2)}) async-start(bf16[8,8,512]{2,1,0:T(8,128)(2,1)} %stack.2), calls=%async_computation | async-start | bytes 131072 | tf_op jit(solution)/shard_map/all_to_all | solution.py:16
  14.6 0.7 copy-start.4
  14.6 43.7 %reduce-scatter.2.cloned.1.call-start = ((), (), s32[]{:S(2)}) async-start(), calls=%async_computation.2 | async-start | bytes 147456 | tf_op jit(solution)/shard_map/reduce_scatter | solution.py:45
  15.3 0.7 copy-start.5
  19.7 0.7 copy-start.3
  20.3 1.9 %copy-start.1 = (bf16[2,512,512]{2,1,0:T(8,128)(2,1)S(1)}, bf16[2,512,512]{2,1,0:T(8,128)(2,1)}, u32[]{:S(2)}) copy-start(bf16[2,512,512]{2,1,0:T(8,128)(2,1)} %get-tuple-element.178) | copy-start | bytes 3145732 | tf_op jit(solution)/shard_map/while
  22.4 1.9 %copy-start.1 = (bf16[2,512,512]{2,1,0:T(8,128)(2,1)S(1)}, bf16[2,512,512]{2,1,0:T(8,128)(2,1)}, u32[]{:S(2)}) copy-start(bf16[2,512,512]{2,1,0:T(8,128)(2,1)} %get-tuple-element.178) | copy-start | bytes 3145732 | tf_op jit(solution)/shard_map/while
  24.6 0.7 copy-start.2
  24.6 54.7 %copy-start.7 = (bf16[2,512,512]{2,1,0:T(8,128)(2,1)}, bf16[2,512,512]{2,1,0:T(8,128)(2,1)S(1)}, u32[]{:S(2)}) copy-start(bf16[2,512,512]{2,1,0:T(8,128)(2,1)S(1)} %get-tuple-element.50) | copy-start | bytes 3145732
Sparse Core Ops, SparseCore 0:
  25.4 32.9 reduce-scatter.1
